TPU v7x, 128 devices: a whole 4x4x4 slice. The times are simulated.
128 devices in a mesh: grp: 8 (over y, core), dom: 16 (over z, x).
Axes of the slice: x: 4, y: 4, z: 4, core: 2. Of those that a mesh axis runs over, the one named last changes fastest.
Arguments:
- diag_blocks: bfloat16 [2048, 384, 384], P(('grp', 'dom')), may hold values from -0.3125 to 0.3125
- face_in: bfloat16 [4096, 384, 384], P(('grp', 'dom')), may hold values from -0.3125 to 0.3125
- face_cross: bfloat16 [2048, 384, 384], P(('grp', 'dom')), may hold values from -0.3125 to 0.3125
- metric: float32 [2048, 384], P(('grp', 'dom')), may hold values from 0.5 to 2
- source_in: int32 [4096], P(('grp', 'dom')), may hold values from 0 to 15
- source_cross: int32 [2048], P(('grp', 'dom')), may hold values from 0 to 15
- orient_in: int32 [4096], P(('grp', 'dom')), may hold values from 0 to 7
- orient_cross: int32 [2048], P(('grp', 'dom')), may hold values from 0 to 7
- peer_in: int32 [4096, 1], P(('grp', 'dom')), may hold values from 0 to 15; in each aligned block of 32 rows (0 to 31, 32 to 63, ...) at most 3 rows name the same one
- peer_cross: int32 [2048, 1], P(('grp', 'dom')), may hold values from 0 to 7; in each aligned block of 16 rows (0 to 15, 16 to 31, ...) at most 3 rows name the same one
- target_in: int32 [4096], P(('grp', 'dom')), may hold values from 0 to 47
- target_cross: int32 [2048], P(('grp', 'dom')), may hold values from 0 to 47
Outputs:
- coarse_diag: float32 [2048, 2304], P('grp')
- coarse_face: float32 [2048, 6912], P('grp')
Inputs may be any that keep to these rules, and one draw needn't show every extreme that they name: `peer_in`: at most 3 records of one device name the same partition; on some device exactly 3 do. `peer_cross`: at most 3 records of one device name the same group; on some device exactly 3 do.
All inputs are finite; a program needn't handle non-finite values.
Results may differ from a plain program's by a relative error of at most 0.0052.
Values may be sent and summed in bfloat16 or wider, within the bound.
A program may use at most 128 MiB of HBM per device.

v0:
```python
import jax
import jax.numpy as jnp
from jax import lax
from jax.sharding import PartitionSpec as P

CROSS_CAP = 3


def corner_table(var_count):
    nodes = -1.0 + 2.0 * jnp.arange(4, dtype=jnp.float32) / 3.0
    basis = jnp.stack(((1.0 - nodes) / 2.0, (1.0 + nodes) / 2.0), axis=1)
    cube = jnp.einsum("ia,jb,kc->abcijk", basis, basis, basis).reshape(8, 64)
    return jnp.kron(jnp.eye(var_count, dtype=jnp.float32), cube)


def restrictor(weights, orient):
    var_count = weights.shape[1] // 64
    table = corner_table(var_count)
    full = weights[:, None, :] * table[None]
    shaped = full.reshape(weights.shape[0], var_count * 8, var_count, 4, 4, 4)
    bits = orient.reshape(-1, 1, 1, 1, 1, 1)
    shaped = jnp.where(bits % 2 == 1, jnp.flip(shaped, 3), shaped)
    shaped = jnp.where(bits // 2 % 2 == 1, jnp.flip(shaped, 4), shaped)
    shaped = jnp.where(bits // 4 % 2 == 1, jnp.flip(shaped, 5), shaped)
    return shaped.reshape(weights.shape[0], var_count * 8, var_count * 64).astype(jnp.bfloat16)


def plain_restrictor(weights):
    table = corner_table(weights.shape[1] // 64)
    return (weights[:, None, :] * table[None]).astype(jnp.bfloat16)


def pick_rows(index, table):
    picks = (index[:, None] == jnp.arange(table.shape[0], dtype=jnp.int32)[None, :]).astype(
        jnp.float32
    )
    return jnp.dot(picks, table, precision=lax.Precision.HIGHEST)


def one_sided(blocks, column_side):
    return jnp.einsum(
        "rcj,rij->rci", column_side, blocks, preferred_element_type=jnp.float32
    ).astype(jnp.bfloat16)


def coarse_terms(row_side, products):
    return jnp.einsum("rci,rdi->rcd", row_side, products, preferred_element_type=jnp.float32)


def id_row(values, width):
    flat = values.reshape(-1).astype(jnp.bfloat16)
    return jnp.pad(flat, (0, width - flat.shape[0]))[None, :]


def per_device(
    diag_blocks,
    face_in,
    face_cross,
    metric,
    source_in,
    source_cross,
    orient_in,
    orient_cross,
    peer_in,
    peer_cross,
    target_in,
    target_cross,
):
    elem_count = metric.shape[0]
    coarse_width = metric.shape[1] // 8
    square = coarse_width * coarse_width
    slots_dev = 3 * elem_count
    group_width = lax.axis_size("dom")
    group_count = lax.axis_size("grp")
    my_dom = lax.axis_index("dom")
    my_grp = lax.axis_index("grp")
    inner_count = face_in.shape[0]
    cross_count = face_cross.shape[0]
    metric_dom = lax.all_gather(metric, "dom", axis=0, tiled=True)
    metric_grp = lax.all_gather(metric, "grp", axis=0, tiled=True)
    diag_side = plain_restrictor(metric)
    diag_c = coarse_terms(diag_side, one_sided(diag_blocks, diag_side))
    diag_rows = diag_c.reshape(elem_count, square).astype(jnp.bfloat16)
    diag_all = lax.all_gather(diag_rows, "dom", axis=0, tiled=True)
    cross_y = one_sided(face_cross, restrictor(pick_rows(source_cross, metric), orient_cross))
    peer_x = peer_cross[:, 0]
    cross_row_side = plain_restrictor(
        pick_rows(peer_x * elem_count + target_cross // 3, metric_grp)
    )
    cross_c = coarse_terms(cross_row_side, cross_y).reshape(cross_count, square)
    cross_ids = jnp.stack((peer_x, target_cross), axis=1)
    cross_packet = jnp.concatenate(
        (cross_c.astype(jnp.bfloat16), id_row(cross_ids, square)), axis=0
    )
    cross_got = lax.all_gather(cross_packet, "grp", axis=0)
    got_rows = cross_got[:, :cross_count, :]
    got_ids = cross_got[:, cross_count, : 2 * cross_count].astype(jnp.int32)
    got_peer = got_ids[:, 0::2]
    got_target = got_ids[:, 1::2]
    match = got_peer == my_grp
    rank = jnp.cumsum(match.astype(jnp.int32), axis=1) - 1
    picks = match[:, None, :] & (
        rank[:, None, :] == jnp.arange(CROSS_CAP, dtype=jnp.int32)[None, :, None]
    )
    mine_rows = (
        jnp.einsum(
            "skr,srq->skq", picks.astype(jnp.bfloat16), got_rows, preferred_element_type=jnp.float32
        )
        .astype(jnp.bfloat16)
        .reshape(group_count * CROSS_CAP, square)
    )
    mine_target = jnp.sum(jnp.where(picks, got_target[:, None, :], 0), axis=2)
    mine_slot = jnp.where(jnp.any(picks, axis=2), my_dom * slots_dev + mine_target, -1).reshape(-1)
    inner_y = one_sided(face_in, restrictor(pick_rows(source_in, metric), orient_in))
    peer_i = peer_in[:, 0]
    inner_row_side = plain_restrictor(pick_rows(peer_i * elem_count + target_in // 3, metric_dom))
    inner_c = coarse_terms(inner_row_side, inner_y).reshape(inner_count, square)
    inner_slot = peer_i * slots_dev + target_in
    slots = jnp.concatenate((inner_slot, mine_slot), axis=0)
    valid = slots >= 0
    slot_code = jnp.stack(
        (jnp.where(valid, slots // 32, -1), jnp.where(valid, slots % 32, 0)), axis=1
    )
    face_packet = jnp.concatenate(
        (inner_c.astype(jnp.bfloat16), mine_rows, id_row(slot_code, square)), axis=0
    )
    face_all = lax.all_gather(face_packet, "dom", axis=0)
    contrib_count = slots.shape[0]
    contrib = face_all[:, :contrib_count, :].reshape(group_width * contrib_count, square)
    codes = face_all[:, contrib_count, : 2 * contrib_count].astype(jnp.int32)
    hi = codes[:, 0::2].reshape(-1)
    lo = codes[:, 1::2].reshape(-1)
    got_slot = jnp.where(hi >= 0, hi * 32 + lo, -1)
    group_slots = group_width * slots_dev
    onehot = (jnp.arange(group_slots, dtype=jnp.int32)[:, None] == got_slot[None, :]).astype(
        jnp.bfloat16
    )
    face = jnp.dot(onehot, contrib, preferred_element_type=jnp.float32)
    coarse_diag = diag_all.astype(jnp.float32)
    coarse_face = face.reshape(group_width * elem_count, 3 * square)
    return (coarse_diag, coarse_face)


def solution(mesh):
    placed = (
        P(("grp", "dom"), None, None),
        P(("grp", "dom"), None, None),
        P(("grp", "dom"), None, None),
        P(("grp", "dom"), None),
        P(("grp", "dom")),
        P(("grp", "dom")),
        P(("grp", "dom")),
        P(("grp", "dom")),
        P(("grp", "dom"), None),
        P(("grp", "dom"), None),
        P(("grp", "dom")),
        P(("grp", "dom")),
    )
    return jax.shard_map(
        per_device,
        mesh=mesh,
        in_specs=placed,
        out_specs=(P("grp", None), P("grp", None)),
        check_vma=False,
    )
```

profile of v0, /device:TPU:1, one launch (start us, length us, event | category | flops | bytes accessed | tf_op | source)
XLA Modules:
  0.0 171.8 jit_solution(11630039760645675383)
XLA Ops:
  7.8 4.3 %fusion.26 = bf16[16,48,48]{2,1,0:T(8,128)(2,1)S(1)} fusion(bf16[16,384,384]{2,1,0:T(8,128)(2,1)} %param.12, f32[48,384]{1,0:T(8,128)S(1)} %mul.191, f32[16,384]{1,0:T(8,128)} %param.15), kind=kOutput, calls=%fused_computation.30 | convolution fusion | flops 256315392 | bytes 4890624 | tf_op jit(solution)/shard_map/rci,rdi->rcd/dot_general | solution.py:47
  12.0 0.9 convert_element_type.104
  13.2 14.6 %all_gather.23 = f32[128,384]{1,0:T(8,128)S(1)} all-gather(f32[16,384]{1,0:T(8,128)S(1)} %copy-done), channel_id=1, replica_groups=mesh['grp'=8,'dom'=16] {'grp'}, dimensions={0}, use_global_device_ids=true | all-gather | bytes 221184 | tf_op jit(solution)/shard_map/all_gather | solution.py:80
  28.6 1.0 broadcast_multiply_fusion.1
  29.6 0.6 reverse_select_fusion.5
  30.2 0.7 reverse_select_fusion.4
  30.9 0.7 fusion.1
  31.8 4.3 %fusion.27 = bf16[16,48,48]{2,1,0:T(8,128)(2,1)S(1)} fusion(bf16[16,384,384]{2,1,0:T(8,128)(2,1)} %param.14, bf16[16,48,384]{1,0,2:T(8,128)(2,1)S(1)} %bitcast.38, f32[16,384]{1,0:T(8,128)S(1)} %fusion.42, f32[48,384]{1,0:T(8,128)S(1)} %mul.191), kind=kOutput, calls=%fused_computation.31 | convolution fusion | flops 255725568 | bytes 5480448 | tf_op jit(solution)/shard_map/rci,rdi->rcd/dot_general | solution.py:47
  36.6 13.5 %all-gather.2 = bf16[8,17,2304]{2,1,0:T(8,128)(2,1)S(1)} all-gather(bf16[1,17,2304]{2,1,0:T(8,128)(2,1)S(1)} %maximum_bitcast_fusion.1), channel_id=2, replica_groups=mesh['grp'=8,'dom'=16] {'grp'}, dimensions={0}, use_global_device_ids=true | all-gather | bytes 705024 | tf_op jit(solution)/shard_map/all_gather | solution.py:95
  50.9 20.3 %all_gather.22 = f32[256,384]{1,0:T(8,128)S(1)} all-gather(f32[16,384]{1,0:T(8,128)S(1)} %copy-done), channel_id=1, replica_groups=mesh['grp'=8,'dom'=16] {'dom'}, dimensions={0}, use_global_device_ids=true | all-gather | bytes 417792 | tf_op jit(solution)/shard_map/all_gather | solution.py:79
  72.0 0.4 fusion.39
  72.4 1.9 %broadcast_multiply_fusion = bf16[32,48,6,4,4,4]{1,0,5,4,3,2:T(8,128)(2,1)S(1)} fusion(f32[48,6,4,4,4]{0,4,3,2,1:T(4,128)S(1)} %broadcast_multiply_fusion.2, f32[32,6,4,4,4]{0,4,3,2,1:T(4,128)S(1)} %bitcast.40), kind=kLoop, calls=%fused_computation.11 | loop fusion | flops 1179648 | bytes 1302528 | tf_op jit(solution)/shard_map/mul | solution.py:19
  74.7 1.3 reverse_select_fusion.2
  76.0 1.5 reverse_select_fusion.1
  77.5 1.1 fusion
  78.6 8.9 %fusion.17 = bf16[32,48,48]{2,1,0:T(8,128)(2,1)} fusion(bf16[32,384,384]{2,1,0:T(8,128)(2,1)} %param.13, bf16[32,48,384]{1,0,2:T(8,128)(2,1)S(1)} %bitcast.37, f32[48,384]{1,0:T(8,128)S(1)} %mul.191, f32[32,384]{1,0:T(8,128)S(1)} %fusion.37), kind=kOutput, calls=%fused_computation.23 | convolution fusion | flops 511451136 | bytes 10887168 | tf_op jit(solution)/shard_map/rci,rdi->rcd/dot_general | solution.py:47
  87.5 1.4 convert_element_type.111
  88.9 0.7 maximum_bitcast_fusion
  89.7 2.8 %convert_element_type.105 = f32[256,2304]{1,0:T(8,128)} convert(bf16[256,2304]{1,0:T(8,128)(2,1)} %all-gather.7.cloned.1.call-done) | non-fusion elementwise | flops 589824 | bytes 3538944 | tf_op jit(solution)/shard_map/convert_element_type | solution.py:139
  92.5 54.4 %all-gather.9.cloned.1.call-done = bf16[16,57,2304]{2,1,0:T(8,128)(2,1)} async-done(((bf16[1,57,2304]{2,1,0:T(8,128)(2,1)}), bf16[16,57,2304]{2,1,0:T(8,128)(2,1)}) %all-gather.9.cloned.1.call-update) | async-done | bytes 4202512 | tf_op jit(solution)/shard_map/all_gather | solution.py:127
  146.9 0.8 slice_convert_fusion
  148.2 2.2 %slice-done = bf16[16,56,2304]{2,1,0:T(8,128)(2,1)S(1)} async-done(((bf16[16,57,2304]{2,1,0:T(8,128)(2,1)}), bf16[16,56,2304]{2,1,0:T(8,128)(2,1)S(1)}, s32[]{:S(2)}) %slice-start) | async-done | bytes 4128792 | tf_op jit(solution)/shard_map/slice | solution.py:129
  150.4 6.0 %fusion.4 = f32[768,2304]{1,0:T(8,128)} fusion(bf16[896,2304]{1,0:T(8,128)(2,1)S(1)} %bitcast.39, s32[896]{0:T(1024)S(1)} %select_n.198), kind=kOutput, calls=%fused_computation.13 | convolution fusion | flops 3171581952 | bytes 11210240 | tf_op jit(solution)/shard_map/dot_general | solution.py:138
  156.3 8.6 %reshape.527 = f32[256,6912]{1,0:T(8,128)} reshape(f32[768,2304]{1,0:T(8,128)} %fusion.4) | data formatting | bytes 14155776 | tf_op jit(solution)/shard_map/reshape | solution.py:140
  (76 shorter events, 4.6 us)
Async XLA Ops:
  7.2 6.0 %copy-start = (f32[16,384]{1,0:T(8,128)S(1)}, f32[16,384]{1,0:T(8,128)}, u32[]{:S(2)}) copy-start(f32[16,384]{1,0:T(8,128)} %param.15) | copy-start | bytes 73732
  7.2 82.5 %all-gather.7.cloned.1.call-start = ((), (), s32[]{:S(2)}) async-start(), calls=%async_computation | async-start | bytes 1253376 | tf_op jit(solution)/shard_map/all_gather | solution.py:84
  7.7 20.4 %copy-start.1 = (s32[16]{0:T(128)S(1)}, s32[16]{0:T(128)}, u32[]{:S(2)}) copy-start(s32[16]{0:T(128)} %param.17) | copy-start | bytes 196
  7.7 20.7 %copy-start.3 = (s32[16]{0:T(128)S(1)}, s32[16]{0:T(128)}, u32[]{:S(2)}) copy-start(s32[16]{0:T(128)} %param.19) | copy-start | bytes 196
  7.7 20.7 %copy-start.5 = (s32[16,1]{0,1:T(1,128)S(1)}, s32[16,1]{0,1:T(1,128)}, u32[]{:S(2)}) copy-start(s32[16,1]{0,1:T(1,128)} %param.21) | copy-start | bytes 196
  7.8 20.8 %copy-start.4 = (s32[16]{0:T(128)S(1)}, s32[16]{0:T(128)}, u32[]{:S(2)}) copy-start(s32[16]{0:T(128)} %param.23) | copy-start | bytes 196
  12.9 134.0 %all-gather.9.cloned.1.call-start = ((), (), s32[]{:S(2)}) async-start(), calls=%async_computation.1 | async-start | bytes 5013504 | tf_op jit(solution)/shard_map/all_gather | solution.py:127
  31.8 39.7 %copy-start.6 = (s32[32]{0:T(128)S(1)}, s32[32]{0:T(128)}, u32[]{:S(2)}) copy-start(s32[32]{0:T(128)} %param.22) | copy-start | bytes 388
  31.8 39.7 %copy-start.7 = (s32[32,1]{0,1:T(1,128)S(1)}, s32[32,1]{0,1:T(1,128)}, u32[]{:S(2)}) copy-start(s32[32,1]{0,1:T(1,128)} %param.20) | copy-start | bytes 388
  31.8 40.2 %copy-start.2 = (s32[32]{0:T(128)S(1)}, s32[32]{0:T(128)}, u32[]{:S(2)}) copy-start(s32[32]{0:T(128)} %param.16) | copy-start | bytes 388
  36.6 37.8 %copy-start.8 = (s32[32]{0:T(128)S(1)}, s32[32]{0:T(128)}, u32[]{:S(2)}) copy-start(s32[32]{0:T(128)} %param.18) | copy-start | bytes 388
  148.2 2.2 %slice-start = ((bf16[16,57,2304]{2,1,0:T(8,128)(2,1)}), bf16[16,56,2304]{2,1,0:T(8,128)(2,1)S(1)}, s32[]{:S(2)}) async-start(bf16[16,57,2304]{2,1,0:T(8,128)(2,1)} %all-gather.9.cloned.1.call-done), calls=%async_computation.2 | async-start | bytes 8257536 | tf_op jit(solution)/shard_map/slice | solution.py:129
Sparse Core Ops, SparseCore 0:
  13.0 44.4 all-gather.6
  89.8 57.1 all-gather.8
where the time goes:
time: 172 us
  waiting for transfers between devices  54.5 us (32%)
  blocking collectives  48.4 us (28%)
  matrix products  24.8 us (14%)
  local copies, waits for them, and re-layouts  15.2 us (9%)
  between operations  14.4 us (8%)
  other arithmetic  14.3 us (8%)
    all_gather x1, waiting for transfers between devices, per_device(): face_all = lax.all_gather(face_packet, 'dom', axis=0)  54.4 us
    all_gather x1, blocking collectives, per_device(): metric_dom = lax.all_gather(metric, 'dom', axis=0, tiled=True)  20.3 us
    dot_general x3, matrix products, coarse_terms(): jnp.einsum('rci,rdi->rcd', row_side, products, preferred_element_type=jnp...  17.4 us
    all_gather x1, blocking collectives, per_device(): metric_grp = lax.all_gather(metric, 'grp', axis=0, tiled=True)  14.6 us
    all_gather x1, blocking collectives, per_device(): cross_got = lax.all_gather(cross_packet, 'grp', axis=0)  13.5 us
    reshape x1, local copies, waits for them, and re-layouts, per_device(): coarse_face = face.reshape(group_width * elem_count, 3 * square)  8.64 us
    dot_general x1, matrix products, per_device(): face = jnp.dot(onehot, contrib, preferred_element_type=jnp.float32)  5.97 us
  transfers between devices with their start and end apart: 2, of which 1 were waited for; matrix products, arithmetic and copies ran while one was open for 18% of the time, Pallas kernels for 0%

commit v1 on v0

--- a/solution.py
+++ b/solution.py
@@ -77,7 +77,9 @@
     inner_count = face_in.shape[0]
     cross_count = face_cross.shape[0]
     metric_dom = lax.all_gather(metric, "dom", axis=0, tiled=True)
-    metric_grp = lax.all_gather(metric, "grp", axis=0, tiled=True)
+    metric_grp = jnp.concatenate(
+        lax.all_to_all(jnp.stack([metric] * lax.axis_size("grp")), "grp", 0, 0), axis=0
+    )
     diag_side = plain_restrictor(metric)
     diag_c = coarse_terms(diag_side, one_sided(diag_blocks, diag_side))
     diag_rows = diag_c.reshape(elem_count, square).astype(jnp.bfloat16)

time: 172 us -> 172 us (level)
  blocking collectives: 48.4 us -> 42 us
  starting transfers between devices: 0.08 us -> 6 us
  waiting for transfers between devices: 54.5 us -> 48.8 us
  other arithmetic: 14.3 us -> 17.4 us
  local copies, waits for them, and re-layouts: 15.2 us -> 17.3 us
    all_gather x1 -> x0, blocking collectives: 14.6 us -> none  [per_device(): metric_grp = lax.all_gather(metric, 'grp', axis=0, tiled=True)]
    all_to_all x0 -> x1, starting transfers between devices: none -> 5.96 us  [per_device(): lax.all_to_all(jnp.stack([metric] * lax.axis_size('grp')), 'grp', 0, 0)]
    all_gather x1, blocking collectives: 13.5 us -> 19.2 us  [per_device(): cross_got = lax.all_gather(cross_packet, 'grp', axis=0)]
    all_gather x1, waiting for transfers between devices: 54.4 us -> 48.8 us  [per_device(): face_all = lax.all_gather(face_packet, 'dom', axis=0)]
    all_gather x1, blocking collectives: 20.3 us -> 22.8 us  [per_device(): metric_dom = lax.all_gather(metric, 'dom', axis=0, tiled=True)]
    select_n x2, other arithmetic: 1.9 us -> 4.05 us  [restrictor(): shaped = jnp.where(bits % 2 == 1, jnp.flip(shaped, 3), shaped)]
  transfers between devices with their start and end apart: 2 -> 3, of which waited for: 1 -> 1; matrix products, arithmetic and copies ran while one was open for 18% -> 23% of each run, Pallas kernels for 0% -> 0%
where the time goes in v1:
time: 172 us; the launch traced here: 171 us
  waiting for transfers between devices  48.8 us (28%)
  blocking collectives  42 us (24%)
  matrix products  24.9 us (14%)
  other arithmetic  17.4 us (10%)
  local copies, waits for them, and re-layouts  17.3 us (10%)
  between operations  14.5 us (8%)
  starting transfers between devices  6 us (3%)
    all_gather x1, waiting for transfers between devices, per_device(): face_all = lax.all_gather(face_packet, 'dom', axis=0)  48.8 us
    all_gather x1, blocking collectives, per_device(): metric_dom = lax.all_gather(metric, 'dom', axis=0, tiled=True)  22.8 us
    all_gather x1, blocking collectives, per_device(): cross_got = lax.all_gather(cross_packet, 'grp', axis=0)  19.2 us
    dot_general x3, matrix products, coarse_terms(): jnp.einsum('rci,rdi->rcd', row_side, products, preferred_element_type=jnp...  17.5 us
    reshape x1, local copies, waits for them, and re-layouts, per_device(): coarse_face = face.reshape(group_width * elem_count, 3 * square)  8.64 us
    dot_general x1, matrix products, per_device(): face = jnp.dot(onehot, contrib, preferred_element_type=jnp.float32)  5.96 us
    all_to_all x1, starting transfers between devices, per_device(): lax.all_to_all(jnp.stack([metric] * lax.axis_size('grp')), 'grp', 0, 0)  5.96 us
    select_n x2, other arithmetic, restrictor(): shaped = jnp.where(bits % 2 == 1, jnp.flip(shaped, 3), shaped)  4.05 us
  transfers between devices with their start and end apart: 3, of which 1 were waited for; matrix products, arithmetic and copies ran while one was open for 23% of the time, Pallas kernels for 0%

profile of v1, /device:TPU:1, one launch (start us, length us, event | category | flops | bytes accessed | tf_op | source)
XLA Modules:
  0.0 170.9 jit_solution(14262000413329774232)
XLA Ops:
  7.2 1.4 stack.14
  8.6 6.0 %all-to-all-start = ((f32[8,16,384]{2,1,0:T(8,128)}), f32[8,16,384]{2,1,0:T(8,128)S(1)}, u32[]{:S(2)}, u32[]{:S(2)}) async-start(f32[8,16,384]{2,1,0:T(8,128)} %stack.14), calls=%async_computation | async-start | bytes 393216 | tf_op jit(solution)/shard_map/all_to_all | solution.py:81
  15.1 4.3 %fusion.26 = bf16[16,48,48]{2,1,0:T(8,128)(2,1)S(1)} fusion(bf16[16,384,384]{2,1,0:T(8,128)(2,1)} %param.12, f32[48,384]{1,0:T(8,128)S(1)} %mul.191, f32[16,384]{1,0:T(8,128)} %param.15), kind=kOutput, calls=%fused_computation.30 | convolution fusion | flops 256315392 | bytes 4890624 | tf_op jit(solution)/shard_map/rci,rdi->rcd/dot_general | solution.py:47
  19.4 0.8 convert_element_type.104
  20.5 22.8 %all_gather.19 = f32[256,384]{1,0:T(8,128)} all-gather(f32[16,384]{1,0:T(8,128)S(1)} %copy-done.1), channel_id=1, replica_groups=mesh['grp'=8,'dom'=16] {'dom'}, dimensions={0}, use_global_device_ids=true | all-gather | bytes 417792 | tf_op jit(solution)/shard_map/all_gather | solution.py:79
  44.7 1.9 %broadcast_multiply_fusion.1 = bf16[16,48,6,4,4,4]{1,0,5,4,3,2:T(8,128)(2,1)} fusion(f32[48,6,4,4,4]{0,4,3,2,1:T(4,128)S(1)} %broadcast_multiply_fusion.2, f32[16,6,4,4,4]{0,4,3,2,1:T(4,128)S(1)} %bitcast.43), kind=kLoop, calls=%fused_computation.17 | loop fusion | flops 589824 | bytes 688128 | tf_op jit(solution)/shard_map/mul | solution.py:19
  46.6 2.1 %broadcast_multiply_fusion = bf16[32,48,6,4,4,4]{1,0,5,4,3,2:T(8,128)(2,1)S(1)} fusion(f32[48,6,4,4,4]{0,4,3,2,1:T(4,128)S(1)} %broadcast_multiply_fusion.2, f32[32,6,4,4,4]{0,4,3,2,1:T(4,128)S(1)} %bitcast.41), kind=kLoop, calls=%fused_computation.11 | loop fusion | flops 1179648 | bytes 1302528 | tf_op jit(solution)/shard_map/mul | solution.py:19
  48.8 1.3 reverse_select_fusion.2
  50.1 1.5 reverse_select_fusion.1
  51.6 1.1 fusion
  53.0 8.9 %fusion.17 = bf16[32,48,48]{2,1,0:T(8,128)(2,1)} fusion(bf16[32,384,384]{2,1,0:T(8,128)(2,1)} %param.13, bf16[32,48,384]{1,0,2:T(8,128)(2,1)S(1)} %bitcast.38, f32[48,384]{1,0:T(8,128)S(1)} %mul.191, f32[32,384]{1,0:T(8,128)S(1)} %fusion.37), kind=kOutput, calls=%fused_computation.23 | convolution fusion | flops 511451136 | bytes 10887168 | tf_op jit(solution)/shard_map/rci,rdi->rcd/dot_general | solution.py:47
  61.9 2.0 %convert_element_type.111 = bf16[32,2304]{1,0:T(8,128)(2,1)} reshape(bf16[32,48,48]{2,1,0:T(8,128)(2,1)} %fusion.17) | data formatting | bytes 294912 | tf_op jit(solution)/shard_map/convert_element_type | solution.py:127
  63.9 2.8 %reverse_select_fusion.5 = bf16[16,48,6,4,4,4]{1,0,5,4,3,2:T(8,128)(2,1)S(1)} fusion(bf16[16,48,6,4,4,4]{1,0,5,4,3,2:T(8,128)(2,1)} %broadcast_multiply_fusion.1, pred[16]{0:T(512)(128)(4,1)S(1)} %get-tuple-element.15), kind=kLoop, calls=%fused_computation.6 | loop fusion | flops 294912 | bytes 1179664 | tf_op jit(solution)/shard_map/jit(_where)/select_n | solution.py:22
  66.7 0.7 reverse_select_fusion.4
  67.4 0.6 fusion.1
  68.2 4.3 %fusion.27 = bf16[16,48,48]{2,1,0:T(8,128)(2,1)S(1)} fusion(bf16[16,384,384]{2,1,0:T(8,128)(2,1)} %param.14, bf16[16,48,384]{1,0,2:T(8,128)(2,1)S(1)} %bitcast.39, f32[16,384]{1,0:T(8,128)S(1)} %fusion.42, f32[48,384]{1,0:T(8,128)S(1)} %mul.191), kind=kOutput, calls=%fused_computation.31 | convolution fusion | flops 255725568 | bytes 5480448 | tf_op jit(solution)/shard_map/rci,rdi->rcd/dot_general | solution.py:47
  72.8 19.2 %all-gather.2 = bf16[8,17,2304]{2,1,0:T(8,128)(2,1)S(1)} all-gather(bf16[1,17,2304]{2,1,0:T(8,128)(2,1)S(1)} %maximum_bitcast_fusion.1), channel_id=2, replica_groups=mesh['grp'=8,'dom'=16] {'grp'}, dimensions={0}, use_global_device_ids=true | all-gather | bytes 705024 | tf_op jit(solution)/shard_map/all_gather | solution.py:97
  93.7 0.7 maximum_bitcast_fusion
  94.5 2.8 %convert_element_type.105 = f32[256,2304]{1,0:T(8,128)} convert(bf16[256,2304]{1,0:T(8,128)(2,1)} %all-gather.7.cloned.1.call-done) | non-fusion elementwise | flops 589824 | bytes 3538944 | tf_op jit(solution)/shard_map/convert_element_type | solution.py:141
  97.3 48.8 %all-gather.9.cloned.1.call-done = bf16[16,57,2304]{2,1,0:T(8,128)(2,1)} async-done(((bf16[1,57,2304]{2,1,0:T(8,128)(2,1)}), bf16[16,57,2304]{2,1,0:T(8,128)(2,1)}) %all-gather.9.cloned.1.call-update) | async-done | bytes 4202512 | tf_op jit(solution)/shard_map/all_gather | solution.py:129
  146.1 0.8 slice_convert_fusion
  147.3 2.2 %slice-done = bf16[16,56,2304]{2,1,0:T(8,128)(2,1)S(1)} async-done(((bf16[16,57,2304]{2,1,0:T(8,128)(2,1)}), bf16[16,56,2304]{2,1,0:T(8,128)(2,1)S(1)}, s32[]{:S(2)}) %slice-start) | async-done | bytes 4128792 | tf_op jit(solution)/shard_map/slice | solution.py:131
  149.5 6.0 %fusion.4 = f32[768,2304]{1,0:T(8,128)} fusion(bf16[896,2304]{1,0:T(8,128)(2,1)S(1)} %bitcast.40, s32[896]{0:T(1024)S(1)} %select_n.198), kind=kOutput, calls=%fused_computation.13 | convolution fusion | flops 3171581952 | bytes 11210240 | tf_op jit(solution)/shard_map/dot_general | solution.py:140
  155.4 8.6 %reshape.533 = f32[256,6912]{1,0:T(8,128)} reshape(f32[768,2304]{1,0:T(8,128)} %fusion.4) | data formatting | bytes 14155776 | tf_op jit(solution)/shard_map/reshape | solution.py:142
  (82 shorter events, 4.9 us)
Async XLA Ops:
  8.6 59.4 %all-to-all-start = ((f32[8,16,384]{2,1,0:T(8,128)}), f32[8,16,384]{2,1,0:T(8,128)S(1)}, u32[]{:S(2)}, u32[]{:S(2)}) async-start(f32[8,16,384]{2,1,0:T(8,128)} %stack.14), calls=%async_computation | async-start | bytes 393216 | tf_op jit(solution)/shard_map/all_to_all | solution.py:81
  14.5 5.9 %copy-start.1 = (f32[16,384]{1,0:T(8,128)S(1)}, f32[16,384]{1,0:T(8,128)}, u32[]{:S(2)}) copy-start(f32[16,384]{1,0:T(8,128)} %param.15) | copy-start | bytes 73732
  14.5 79.9 %all-gather.7.cloned.1.call-start = ((), (), s32[]{:S(2)}) async-start(), calls=%async_computation.1 | async-start | bytes 1253376 | tf_op jit(solution)/shard_map/all_gather | solution.py:86
  15.0 28.5 %copy-start.3 = (s32[16]{0:T(128)S(1)}, s32[16]{0:T(128)}, u32[]{:S(2)}) copy-start(s32[16]{0:T(128)} %param.17) | copy-start | bytes 196
  15.1 28.9 %copy-start.5 = (s32[16]{0:T(128)S(1)}, s32[16]{0:T(128)}, u32[]{:S(2)}) copy-start(s32[16]{0:T(128)} %param.19) | copy-start | bytes 196
  15.1 28.9 %copy-start.7 = (s32[16,1]{0,1:T(1,128)S(1)}, s32[16,1]{0,1:T(1,128)}, u32[]{:S(2)}) copy-start(s32[16,1]{0,1:T(1,128)} %param.21) | copy-start | bytes 196
  15.1 28.9 %copy-start.6 = (s32[16]{0:T(128)S(1)}, s32[16]{0:T(128)}, u32[]{:S(2)}) copy-start(s32[16]{0:T(128)} %param.23) | copy-start | bytes 196
  15.1 29.2 %copy-start.4 = (s32[32]{0:T(128)S(1)}, s32[32]{0:T(128)}, u32[]{:S(2)}) copy-start(s32[32]{0:T(128)} %param.16) | copy-start | bytes 388
  20.3 125.8 %all-gather.9.cloned.1.call-start = ((), (), s32[]{:S(2)}) async-start(), calls=%async_computation.2 | async-start | bytes 5013504 | tf_op jit(solution)/shard_map/all_gather | solution.py:129
  43.4 5.3 %copy-start.8 = (s32[32]{0:T(128)S(1)}, s32[32]{0:T(128)}, u32[]{:S(2)}) copy-start(s32[32]{0:T(128)} %param.18) | copy-start | bytes 388
  43.4 5.3 %copy-start.9 = (s32[32]{0:T(128)S(1)}, s32[32]{0:T(128)}, u32[]{:S(2)}) copy-start(s32[32]{0:T(128)} %param.22) | copy-start | bytes 388
  43.4 5.3 %copy-start.10 = (s32[32,1]{0,1:T(1,128)S(1)}, s32[32,1]{0,1:T(1,128)}, u32[]{:S(2)}) copy-start(s32[32,1]{0,1:T(1,128)} %param.20) | copy-start | bytes 388
  51.6 1.2 copy-start
  68.2 25.4 %copy-start.2 = (bf16[32,2304]{1,0:T(8,128)(2,1)S(1)}, bf16[32,2304]{1,0:T(8,128)(2,1)}, u32[]{:S(2)}) copy-start(bf16[32,2304]{1,0:T(8,128)(2,1)} %convert_element_type.111) | copy-start | bytes 442372
  147.3 2.2 %slice-start = ((bf16[16,57,2304]{2,1,0:T(8,128)(2,1)}), bf16[16,56,2304]{2,1,0:T(8,128)(2,1)S(1)}, s32[]{:S(2)}) async-start(bf16[16,57,2304]{2,1,0:T(8,128)(2,1)} %all-gather.9.cloned.1.call-done), calls=%async_computation.3 | async-start | bytes 8257536 | tf_op jit(solution)/shard_map/slice | solution.py:131
Sparse Core Ops, SparseCore 0:
  20.4 43.2 all-gather.6
  94.5 51.4 all-gather.8
